TPU v7x, 32 devices: a whole 2x2x4 slice. The times are simulated.
32 devices in a mesh: groups: 2 (over x), tile: 16 (over z, y, core).
Axes of the slice: x: 2, y: 2, z: 4, core: 2. Of those that a mesh axis runs over, the one named last changes fastest.
Arguments:
- probes: float32 [8, 262144], P(None, ('groups', 'tile')), parts along dimension 1, may hold values from -6 to 6
- level_set: float32 [262144], P(('groups', 'tile')), parts along dimension 0, may hold values from -6 to 6
- unit_label: int32 [262144], P(('groups', 'tile')), parts along dimension 0, may hold values from 0 to 3
- contrast: float32 [8], P('groups'), parts along dimension 0, may hold values from 0.2 to 1.5
- station_weight: float32 [65536], P('groups'), parts along dimension 0, may hold values from 0.2 to 2
- u_factor: bfloat16 [4096, 32, 512], P(('groups', 'tile')), parts along dimension 0, may hold values from -1 to 1
- v_factor: bfloat16 [4096, 32, 512], P(('groups', 'tile')), parts along dimension 0, may hold values from -0.25 to 0.25
- col_owner: int32 [4096, 1], P('groups'), parts along dimension 0, may hold values from 0 to 15; in each aligned block of 128 rows (0 to 127, 128 to 255, ...) at most 16 rows name the same one
- col_local: int32 [4096], P('groups'), parts along dimension 0, may hold values from 0 to 15
- row_owner: int32 [4096, 1], P('groups'), parts along dimension 0, may hold values from 0 to 15; in each aligned block of 128 rows (0 to 127, 128 to 255, ...) at most 16 rows name the same one
- row_local: int32 [4096], P('groups'), parts along dimension 0, may hold values from 0 to 3
- tile_rank: int32 [4096], P('groups'), parts along dimension 0, may hold values from 8 to 32
Outputs:
- hessian_probes: float32 [8, 262144], P(None, ('groups', 'tile')), parts along dimension 1
There are 2 independent parts, one for each index of `groups`. A program takes and returns all parts, laid end to end along the dimension named above; each array names one. Nothing has to cross between parts.
Inputs may be any that keep to these rules, and one draw needn't show every extreme that they name: `col_owner`: among the 128 tiles of one device (aligned blocks of 128 entries) no owner is named more than 16 times, a bound that some block reaches. `row_owner`: among the 128 tiles of one device (aligned blocks of 128 entries) no owner is named more than 16 times, a bound that some block reaches.
All inputs are finite; a program needn't handle non-finite values.
Results may differ from a plain program's by a relative error of at most 0.005.
Values may be sent and summed in bfloat16 or wider, within the bound.
No kernel may reach another device: no remote copies, remote signals or barrier semaphores. Data moves between devices by JAX's collectives and lax.ppermute only.
A program may use at most 64 MiB of HBM per device.

v0:
```python
import jax
import jax.numpy as jnp
from jax import lax
from jax.sharding import PartitionSpec as P

HIGHEST = lax.Precision.HIGHEST


def rank_within(owner_table, target, capacity):
    matches = (owner_table == target).astype(jnp.int32)
    position = jnp.cumsum(matches, axis=-1) - 1
    slot_ids = jnp.arange(capacity, dtype=jnp.int32)
    chosen = (matches[:, None, :] == 1) & (position[:, None, :] == slot_ids[None, :, None])
    return chosen.astype(jnp.float32)


def sender_table(owner_table, local_table, target, capacity, block_count):
    chosen = rank_within(owner_table, target, capacity)
    local_match = (
        local_table[:, :, None] == jnp.arange(block_count, dtype=jnp.int32)[None, None, :]
    ).astype(jnp.float32)
    return jnp.einsum(
        "pqs,psb->pqb", chosen, local_match, precision=HIGHEST, preferred_element_type=jnp.float32
    )


def receiver_table(owner_mine, capacity, peer_count):
    count = owner_mine.shape[0]
    positions = jnp.arange(count, dtype=jnp.int32)
    earlier = (owner_mine[None, :] == owner_mine[:, None]) & (
        positions[None, :] < positions[:, None]
    )
    order = jnp.sum(earlier.astype(jnp.int32), axis=1)
    target = owner_mine * capacity + order
    return (target[:, None] == jnp.arange(peer_count * capacity, dtype=jnp.int32)[None, :]).astype(
        jnp.float32
    )


def shards(
    probes,
    level_set,
    unit_label,
    contrast,
    station_weight,
    u_factor,
    v_factor,
    col_owner,
    col_local,
    row_owner,
    row_local,
    tile_rank,
):
    peer_count = lax.axis_size("tile")
    own_index = lax.axis_index("tile")
    tile_count, rank_max, station_width = u_factor.shape
    cell_width = v_factor.shape[2]
    probe_count, cell_total = probes.shape
    cell_blocks = cell_total // cell_width
    station_blocks = station_weight.shape[0] // (peer_count * station_width)
    capacity = max(2, 2 * tile_count // peer_count)
    flat_cells = probe_count * cell_width
    flat_stations = probe_count * station_width
    col_owner_all = col_owner.reshape(peer_count, tile_count)
    col_local_all = col_local.reshape(peer_count, tile_count)
    row_owner_all = row_owner.reshape(peer_count, tile_count)
    row_local_all = row_local.reshape(peer_count, tile_count)
    col_owner_mine = lax.dynamic_index_in_dim(col_owner_all, own_index, 0, keepdims=False)
    col_local_mine = lax.dynamic_index_in_dim(col_local_all, own_index, 0, keepdims=False)
    row_owner_mine = lax.dynamic_index_in_dim(row_owner_all, own_index, 0, keepdims=False)
    row_local_mine = lax.dynamic_index_in_dim(row_local_all, own_index, 0, keepdims=False)
    rank_mine = lax.dynamic_index_in_dim(
        tile_rank.reshape(peer_count, tile_count), own_index, 0, keepdims=False
    )
    unit_count = contrast.shape[0]
    unit_match = (unit_label[None, :] == jnp.arange(unit_count, dtype=jnp.int32)[:, None]).astype(
        jnp.float32
    )
    scaling = jnp.sum(unit_match * contrast[:, None], axis=0) / (1.0 + level_set * level_set)
    scaled = (probes * scaling[None, :]).astype(jnp.bfloat16)
    cell_rows = (
        scaled.reshape(probe_count, cell_blocks, cell_width)
        .transpose(1, 0, 2)
        .reshape(cell_blocks, flat_cells)
    )
    col_global = col_owner_mine * cell_blocks + col_local_mine
    col_slots = receiver_table(col_owner_mine, capacity, peer_count)
    col_choice = sender_table(col_owner_all, col_local_all, own_index, capacity, cell_blocks)
    piece = lax.all_gather(cell_rows, "tile", axis=0, tiled=True)
    rows_here = piece.shape[0]
    match = (col_global[:, None] == jnp.arange(rows_here, dtype=jnp.int32)[None, :]).astype(
        jnp.bfloat16
    )
    fetched = jnp.dot(match, piece, preferred_element_type=jnp.float32)
    tile_cells = fetched.astype(jnp.bfloat16).reshape(tile_count, probe_count, cell_width)
    keep = (jnp.arange(rank_max, dtype=jnp.int32)[None, :] < rank_mine[:, None]).astype(
        jnp.float32
    )[:, None, :]
    coeff = jnp.einsum("tkc,trc->tkr", tile_cells, v_factor, preferred_element_type=jnp.float32)
    coeff = (coeff * keep).astype(jnp.bfloat16)
    partial_value = jnp.einsum(
        "tkr,trs->tks", coeff, u_factor, preferred_element_type=jnp.float32
    ).reshape(tile_count, flat_stations)
    row_global = row_owner_mine * station_blocks + row_local_mine
    match = (
        jnp.arange(station_blocks * lax.axis_size("tile"), dtype=jnp.int32)[:, None]
        == row_global[None, :]
    ).astype(jnp.float32)
    predicted = lax.psum_scatter(
        jnp.dot(match, partial_value, precision=HIGHEST, preferred_element_type=jnp.float32),
        "tile",
        scatter_dimension=0,
        tiled=True,
    )
    weight_mine = lax.dynamic_slice_in_dim(
        station_weight, own_index * station_blocks * station_width, station_blocks * station_width
    )
    weighted = (
        predicted.reshape(station_blocks, probe_count, station_width)
        * weight_mine.reshape(station_blocks, 1, station_width)
    ).astype(jnp.bfloat16)
    weighted = weighted.reshape(station_blocks, flat_stations)
    row_choice = sender_table(row_owner_all, row_local_all, own_index, capacity, station_blocks)
    outgoing_data = jnp.einsum(
        "pqb,bf->pqf", row_choice.astype(jnp.bfloat16), weighted, preferred_element_type=jnp.float32
    ).astype(jnp.bfloat16)
    incoming_data = lax.all_to_all(outgoing_data, "tile", split_axis=0, concat_axis=0, tiled=True)
    row_slots = receiver_table(row_owner_mine, capacity, peer_count)
    tile_data = jnp.dot(
        row_slots.astype(jnp.bfloat16),
        incoming_data.reshape(peer_count * capacity, flat_stations),
        preferred_element_type=jnp.float32,
    )
    tile_weighted = tile_data.astype(jnp.bfloat16).reshape(tile_count, probe_count, station_width)
    back = jnp.einsum("tks,trs->tkr", tile_weighted, u_factor, preferred_element_type=jnp.float32)
    back = (back * keep).astype(jnp.bfloat16)
    spread = jnp.einsum("tkr,trc->tkc", back, v_factor, preferred_element_type=jnp.float32).reshape(
        tile_count, flat_cells
    )
    slot_rows = col_slots.T.reshape(peer_count, capacity, tile_count)
    returned = jnp.einsum(
        "pqt,tf->pqf", slot_rows, spread, precision=HIGHEST, preferred_element_type=jnp.float32
    )
    arrived = lax.all_to_all(returned, "tile", split_axis=0, concat_axis=0, tiled=True)
    summed = jnp.einsum(
        "pqb,pqf->bf", col_choice, arrived, precision=HIGHEST, preferred_element_type=jnp.float32
    )
    gradient = (
        summed.reshape(cell_blocks, probe_count, cell_width)
        .transpose(1, 0, 2)
        .reshape(probe_count, cell_total)
    )
    return scaling[None, :] * gradient


def solution(mesh):
    placed = (
        P(None, ("groups", "tile")),
        P(("groups", "tile")),
        P(("groups", "tile")),
        P("groups"),
        P("groups"),
        P(("groups", "tile"), None, None),
        P(("groups", "tile"), None, None),
        P("groups", None),
        P("groups"),
        P("groups", None),
        P("groups"),
        P("groups"),
    )
    return jax.shard_map(
        shards, mesh=mesh, in_specs=placed, out_specs=P(None, ("groups", "tile")), check_vma=False
    )
```

profile of v0, /device:TPU:13, one launch (start us, length us, event | category | flops | bytes accessed | tf_op | source)
XLA Modules:
  0.0 335.7 jit_solution(17233125049416313303)
XLA Ops:
  6.5 0.9 select_reduce_fusion
  7.5 0.8 add_divide_fusion
  8.2 1.0 multiply_convert_fusion
  9.2 0.7 copy.15
  10.0 0.7 dynamic_slice.24
  10.7 0.7 fusion.35
  11.4 0.7 fusion.38
  12.3 38.9 %all-gather.2.cloned.1.call-done = bf16[256,4096]{1,0:T(8,128)(2,1)} async-done(((bf16[16,4096]{1,0:T(8,128)(2,1)}), bf16[256,4096]{1,0:T(8,128)(2,1)}) %all-gather.2.cloned.1.call-update) | async-done | bytes 2097168 | tf_op jit(solution)/shard_map/all_gather | solution.py:89
  51.2 2.1 convolution_convert_fusion.2
  53.2 0.4 copy.16
  53.6 5.2 %fusion.3 = f32[128,8,512]{2,1,0:T(8,128)S(1)} fusion(bf16[128,32,512]{2,1,0:T(8,128)(2,1)} %param.17, bf16[128,8,512]{2,1,0:T(8,128)(2,1)S(1)} %bitcast.63, bf16[128,32,512]{2,1,0:T(8,128)(2,1)} %param.18, f32[128,32]{1,0:T(8,128)S(1)} %fusion.23), kind=kOutput, calls=%fused_computation.8 | convolution fusion | flops 67174400 | bytes 11550720 | tf_op jit(solution)/shard_map/tkr,trs->tks/dot_general | solution.py:101
  58.8 1.6 copy.17
  60.5 1.9 fusion.28
  62.5 0.3 reduce_window_sum.18
  62.8 0.6 dynamic-slice
  64.3 89.8 %all-reduce.3.cloned.1.call-done = f32[64,4096]{1,0:T(8,128)} async-done(((f32[64,4096]{1,0:T(8,128)}), f32[64,4096]{1,0:T(8,128)}) %all-reduce.3.cloned.1.call-update) | async-done | bytes 1048592
  154.0 3.1 convolution_convert_fusion
  157.1 6.8 %all-to-all-start = ((bf16[16,16,4096]{2,1,0:T(8,128)(2,1)}), bf16[16,16,4096]{2,1,0:T(8,128)(2,1)S(1)}, u32[]{:S(2)}, u32[]{:S(2)}) async-start(bf16[16,16,4096]{2,1,0:T(8,128)(2,1)} %convolution_convert_fusion), calls=%async_computation | async-start | bytes 4194304 | tf_op jit(solution)/shard_map/all_to_all | solution.py:127
  163.9 0.2 convert_reduce_fusion
  164.0 0.2 convert_reduce_fusion.1
  164.3 47.0 %all-to-all-done = bf16[16,16,4096]{2,1,0:T(8,128)(2,1)S(1)} async-done(((bf16[16,16,4096]{2,1,0:T(8,128)(2,1)}), bf16[16,16,4096]{2,1,0:T(8,128)(2,1)S(1)}, u32[]{:S(2)}, u32[]{:S(2)}) %all-to-all-start) | async-done | bytes 2097184 | tf_op jit(solution)/shard_map/all_to_all | solution.py:127
  211.3 0.5 convolution_convert_fusion.1
  211.8 0.4 copy.19
  212.2 6.5 %fusion.2 = f32[128,8,512]{2,1,0:T(8,128)} fusion(bf16[128,32,512]{2,1,0:T(8,128)(2,1)} %param.18, bf16[128,8,512]{2,1,0:T(8,128)(2,1)S(1)} %bitcast.62, bf16[128,32,512]{2,1,0:T(8,128)(2,1)} %param.17, f32[128,32]{1,0:T(8,128)S(1)} %fusion.23), kind=kOutput, calls=%fused_computation.7 | convolution fusion | flops 67174400 | bytes 11550720 | tf_op jit(solution)/shard_map/tkr,trc->tkc/dot_general | solution.py:137
  218.7 1.7 reshape.169
  220.5 3.8 %fusion.11 = f32[16,16,4096]{2,1,0:T(8,128)} fusion(f32[128,4096,1]{1,0,2:T(8,128)S(1)} %reshape.169, s32[16,16]{1,0:T(8,128)S(1)} %multiply_add_fusion, s32[128]{0:T(128)S(1)} %multiply_add_fusion.2), kind=kOutput, calls=%fused_computation.25 | convolution fusion | flops 1610645504 | bytes 6292992 | tf_op jit(solution)/shard_map/pqt,tf->pqf/dot_general | solution.py:141
  224.3 5.0 %all-to-all-start.1 = ((f32[16,16,4096]{2,1,0:T(8,128)}), f32[16,16,4096]{2,1,0:T(8,128)}, u32[]{:S(2)}, u32[]{:S(2)}) async-start(f32[16,16,4096]{2,1,0:T(8,128)} %fusion.11), calls=%async_computation.1 | async-start | bytes 8388608 | tf_op jit(solution)/shard_map/all_to_all | solution.py:144
  229.4 0.3 reduce_window_sum.17
  229.7 0.2 fusion.7
  229.8 92.0 %all-to-all-done.1 = f32[16,16,4096]{2,1,0:T(8,128)} async-done(((f32[16,16,4096]{2,1,0:T(8,128)}), f32[16,16,4096]{2,1,0:T(8,128)}, u32[]{:S(2)}, u32[]{:S(2)}) %all-to-all-start.1) | async-done | bytes 4194336 | tf_op jit(solution)/shard_map/all_to_all | solution.py:144
  321.8 6.2 %fusion.40 = f32[16,4096,1]{1,0,2:T(8,128)S(1)} fusion(f32[16,16,16]{1,2,0:T(8,128)S(1)} %fusion.7, f32[16,16,4096]{2,1,0:T(8,128)} %all-to-all-done.1), kind=kOutput, calls=%fused_computation.75 | convolution fusion | flops 201326592 | bytes 4472832 | tf_op jit(solution)/shard_map/pqb,pqf->bf/dot_general | solution.py:145
  328.2 0.7 broadcast_multiply_fusion
  (26 shorter events, 0.6 us)
Async XLA Ops:
  6.5 44.6 %all-gather.2.cloned.1.call-start = ((), (), s32[]{:S(2)}) async-start(), calls=%async_computation.2 | async-start | bytes 2228224 | tf_op jit(solution)/shard_map/all_gather | solution.py:89
  10.0 144.1 %all-reduce.3.cloned.1.call-start = ((), (), s32[]{:S(2)}) async-start(), calls=%async_computation.3 | async-start | bytes 2097152
  60.5 2.0 copy-start.1
  60.5 2.0 copy-start.2
  60.5 2.3 copy-start.4
  60.5 3.6 %copy-start.3 = (s32[2048]{0:T(1024)S(1)}, s32[2048]{0:T(1024)}, u32[]{:S(2)}) copy-start(s32[2048]{0:T(1024)} %param.22) | copy-start | bytes 24580
  157.1 54.2 %all-to-all-start = ((bf16[16,16,4096]{2,1,0:T(8,128)(2,1)}), bf16[16,16,4096]{2,1,0:T(8,128)(2,1)S(1)}, u32[]{:S(2)}, u32[]{:S(2)}) async-start(bf16[16,16,4096]{2,1,0:T(8,128)(2,1)} %convolution_convert_fusion), calls=%async_computation | async-start | bytes 4194304 | tf_op jit(solution)/shard_map/all_to_all | solution.py:127
  224.3 5.3 %copy-start = (s32[2048]{0:T(1024)S(1)}, s32[2048]{0:T(1024)}, u32[]{:S(2)}) copy-start(s32[2048]{0:T(1024)} %param.20) | copy-start | bytes 24580
  224.3 97.5 %all-to-all-start.1 = ((f32[16,16,4096]{2,1,0:T(8,128)}), f32[16,16,4096]{2,1,0:T(8,128)}, u32[]{:S(2)}, u32[]{:S(2)}) async-start(f32[16,16,4096]{2,1,0:T(8,128)} %fusion.11), calls=%async_computation.1 | async-start | bytes 8388608 | tf_op jit(solution)/shard_map/all_to_all | solution.py:144
Sparse Core Ops, SparseCore 0:
  10.1 41.0 all-gather.1
  62.6 91.4 all-reduce.2
where the time goes:
time: 336 us
  waiting for transfers between devices  268 us (80%)
  matrix products  29.6 us (9%)
  between operations  14.3 us (4%)
  starting transfers between devices  11.8 us (4%)
  local copies, waits for them, and re-layouts  6.41 us (2%)
  other arithmetic  5.89 us (2%)
    all_to_all x1, waiting for transfers between devices, shards(): lax.all_to_all(returned, 'tile', split_axis=0, concat_axis=0, tiled=True)  92 us
    unnamed x3, waiting for transfers between devices  89.8 us
    all_to_all x1, waiting for transfers between devices, shards(): lax.all_to_all(outgoing_data, 'tile', split_axis=0, concat_axis=0, tiled=...  47 us
    all_gather x1, waiting for transfers between devices, shards(): piece = lax.all_gather(cell_rows, 'tile', axis=0, tiled=True)  38.9 us
    all_to_all x1, starting transfers between devices, shards(): lax.all_to_all(outgoing_data, 'tile', split_axis=0, concat_axis=0, tiled=...  6.76 us
  transfers between devices with their start and end apart: 4, of which 4 were waited for; matrix products, arithmetic and copies ran while one was open for 1% of the time, Pallas kernels for 0%

commit v1 on v0

--- a/solution.py
+++ b/solution.py
@@ -86,7 +86,25 @@
     col_global = col_owner_mine * cell_blocks + col_local_mine
     col_slots = receiver_table(col_owner_mine, capacity, peer_count)
     col_choice = sender_table(col_owner_all, col_local_all, own_index, capacity, cell_blocks)
-    piece = lax.all_gather(cell_rows, "tile", axis=0, tiled=True)
+    size, index, extent = (lax.axis_size("tile"), lax.axis_index("tile"), cell_rows.shape[0])
+    right = [(i, (i + 1) % size) for i in range(size)]
+    left = [(i, (i - 1) % size) for i in range(size)]
+    piece = jnp.zeros(
+        (*cell_rows.shape[:0], size * extent, *cell_rows.shape[0 + 1 :]), cell_rows.dtype
+    )
+    piece = lax.dynamic_update_slice_in_dim(piece, cell_rows, index * extent, axis=0)
+    from_left = from_right = cell_rows
+    half = size // 2
+    for step in range(1, half + 1):
+        from_left = lax.ppermute(from_left, "tile", right)
+        piece = lax.dynamic_update_slice_in_dim(
+            piece, from_left, (index - step) % size * extent, axis=0
+        )
+        if step < size - half:
+            from_right = lax.ppermute(from_right, "tile", left)
+            piece = lax.dynamic_update_slice_in_dim(
+                piece, from_right, (index + step) % size * extent, axis=0
+            )
     rows_here = piece.shape[0]
     match = (col_global[:, None] == jnp.arange(rows_here, dtype=jnp.int32)[None, :]).astype(
         jnp.bfloat16

time: 336 us -> 347 us (1.033)
  starting transfers between devices: 11.8 us -> 37.5 us
  waiting for transfers between devices: 268 us -> 255 us
    all_gather x1 -> x0, waiting for transfers between devices: 38.9 us -> none  [shards(): piece = lax.all_gather(cell_rows, 'tile', axis=0, tiled=True)]
    ppermute x0 -> x15, starting transfers between devices: none -> 25.8 us  [the longest x8 25.8 us: shards(): from_left = lax.ppermute(from_left, 'tile', right)]
    ppermute x0 -> x15, waiting for transfers between devices: none -> 13.3 us  [the longest x8 13.3 us: shards(): from_left = lax.ppermute(from_left, 'tile', right)]
    unnamed x3 -> x2, waiting for transfers between devices: 89.8 us -> 103 us
  transfers between devices with their start and end apart: 4 -> 18, of which waited for: 4 -> 10; matrix products, arithmetic and copies ran while one was open for 1% -> 1% of each run, Pallas kernels for 0% -> 0%
where the time goes in v1:
time: 347 us; the launch traced here: 346 us
  waiting for transfers between devices  255 us (73%)
  starting transfers between devices  37.5 us (11%)
  matrix products  28 us (8%)
  between operations  14.6 us (4%)
  local copies, waits for them, and re-layouts  6.21 us (2%)
  other arithmetic  5.18 us (1%)
    unnamed x2, waiting for transfers between devices  103 us
    all_to_all x1, waiting for transfers between devices, shards(): lax.all_to_all(returned, 'tile', split_axis=0, concat_axis=0, tiled=True)  92 us
    all_to_all x1, waiting for transfers between devices, shards(): lax.all_to_all(outgoing_data, 'tile', split_axis=0, concat_axis=0, tiled=...  47 us
    ppermute x8, starting transfers between devices, shards(): from_left = lax.ppermute(from_left, 'tile', right)  25.8 us
    ppermute x8, waiting for transfers between devices, shards(): from_left = lax.ppermute(from_left, 'tile', right)  13.3 us
  transfers between devices with their start and end apart: 18, of which 10 were waited for; matrix products, arithmetic and copies ran while one was open for 1% of the time, Pallas kernels for 0%

profile of v1, /device:TPU:13, one launch (start us, length us, event | category | flops | bytes accessed | tf_op | source)
XLA Modules:
  0.0 346.4 jit_solution(1906103821012045004)
XLA Ops:
  6.6 0.9 select_reduce_fusion
  7.5 0.8 add_divide_fusion
  8.3 1.0 multiply_convert_fusion
  9.3 1.9 collective-permute-start
  13.3 3.2 collective-permute-start.2
  16.6 1.9 collective-permute-done.2
  18.5 3.4 collective-permute-start.4
  22.0 1.9 collective-permute-done.4
  23.9 3.4 collective-permute-start.6
  27.4 1.9 collective-permute-done.6
  29.3 3.4 collective-permute-start.8
  32.8 1.9 collective-permute-done.8
  34.7 3.4 collective-permute-start.10
  38.2 1.9 collective-permute-done.10
  40.1 3.4 collective-permute-start.12
  43.6 1.9 collective-permute-done.12
  45.5 3.4 collective-permute-start.14
  49.0 1.9 collective-permute-done.14
  51.8 5.2 %fusion.3 = f32[128,8,512]{2,1,0:T(8,128)S(1)} fusion(bf16[128,32,512]{2,1,0:T(8,128)(2,1)} %param.17, bf16[128,8,512]{2,1,0:T(8,128)(2,1)S(1)} %bitcast.63, bf16[128,32,512]{2,1,0:T(8,128)(2,1)} %param.18, f32[128,32]{1,0:T(8,128)S(1)} %fusion.23), kind=kOutput, calls=%fused_computation.8 | convolution fusion | flops 67174400 | bytes 11550720 | tf_op jit(solution)/shard_map/tkr,trs->tks/dot_general | solution.py:119
  57.0 1.6 copy.17
  58.6 1.9 fusion.28
  62.3 102.6 %all-reduce.3.cloned.1.call-done = f32[64,4096]{1,0:T(8,128)} async-done(((f32[64,4096]{1,0:T(8,128)}), f32[64,4096]{1,0:T(8,128)}) %all-reduce.3.cloned.1.call-update) | async-done | bytes 1048592
  164.9 3.1 convolution_convert_fusion
  167.9 6.8 %all-to-all-start = ((bf16[16,16,4096]{2,1,0:T(8,128)(2,1)}), bf16[16,16,4096]{2,1,0:T(8,128)(2,1)S(1)}, u32[]{:S(2)}, u32[]{:S(2)}) async-start(bf16[16,16,4096]{2,1,0:T(8,128)(2,1)} %convolution_convert_fusion), calls=%async_computation | async-start | bytes 4194304 | tf_op jit(solution)/shard_map/all_to_all | solution.py:145
  175.1 47.0 %all-to-all-done = bf16[16,16,4096]{2,1,0:T(8,128)(2,1)S(1)} async-done(((bf16[16,16,4096]{2,1,0:T(8,128)(2,1)}), bf16[16,16,4096]{2,1,0:T(8,128)(2,1)S(1)}, u32[]{:S(2)}, u32[]{:S(2)}) %all-to-all-start) | async-done | bytes 2097184 | tf_op jit(solution)/shard_map/all_to_all | solution.py:145
  223.0 6.5 %fusion.2 = f32[128,8,512]{2,1,0:T(8,128)} fusion(bf16[128,32,512]{2,1,0:T(8,128)(2,1)} %param.18, bf16[128,8,512]{2,1,0:T(8,128)(2,1)S(1)} %bitcast.62, bf16[128,32,512]{2,1,0:T(8,128)(2,1)} %param.17, f32[128,32]{1,0:T(8,128)S(1)} %fusion.23), kind=kOutput, calls=%fused_computation.7 | convolution fusion | flops 67174400 | bytes 11550720 | tf_op jit(solution)/shard_map/tkr,trc->tkc/dot_general | solution.py:155
  229.6 1.7 reshape.169
  231.3 3.8 %fusion.11 = f32[16,16,4096]{2,1,0:T(8,128)} fusion(f32[128,4096,1]{1,0,2:T(8,128)S(1)} %reshape.169, s32[16,16]{1,0:T(8,128)S(1)} %multiply_add_fusion, s32[128]{0:T(128)S(1)} %multiply_add_fusion.2), kind=kOutput, calls=%fused_computation.25 | convolution fusion | flops 1610645504 | bytes 6292992 | tf_op jit(solution)/shard_map/pqt,tf->pqf/dot_general | solution.py:159
  235.1 4.9 %all-to-all-start.1 = ((f32[16,16,4096]{2,1,0:T(8,128)}), f32[16,16,4096]{2,1,0:T(8,128)}, u32[]{:S(2)}, u32[]{:S(2)}) async-start(f32[16,16,4096]{2,1,0:T(8,128)} %fusion.11), calls=%async_computation.1 | async-start | bytes 8388608 | tf_op jit(solution)/shard_map/all_to_all | solution.py:162
  240.5 92.0 %all-to-all-done.1 = f32[16,16,4096]{2,1,0:T(8,128)} async-done(((f32[16,16,4096]{2,1,0:T(8,128)}), f32[16,16,4096]{2,1,0:T(8,128)}, u32[]{:S(2)}, u32[]{:S(2)}) %all-to-all-start.1) | async-done | bytes 4194336 | tf_op jit(solution)/shard_map/all_to_all | solution.py:162
  332.5 6.2 %fusion.40 = f32[16,4096,1]{1,0,2:T(8,128)S(1)} fusion(f32[16,16,16]{1,2,0:T(8,128)S(1)} %fusion.7, f32[16,16,4096]{2,1,0:T(8,128)} %all-to-all-done.1), kind=kOutput, calls=%fused_computation.91 | convolution fusion | flops 201326592 | bytes 4472832 | tf_op jit(solution)/shard_map/pqb,pqf->bf/dot_general | solution.py:163
  338.8 0.7 broadcast_multiply_fusion
  (70 shorter events, 5.9 us)
Async XLA Ops:
  6.5 5.6 %copy-start.1 = (s32[2048,1]{0,1:T(1,128)S(1)}, s32[2048,1]{0,1:T(1,128)}, u32[]{:S(2)}) copy-start(s32[2048,1]{0,1:T(1,128)} %param.21) | copy-start | bytes 24580
  6.5 5.6 %copy-start.3 = (s32[2048]{0:T(1024)S(1)}, s32[2048]{0:T(1024)}, u32[]{:S(2)}) copy-start(s32[2048]{0:T(1024)} %param.22) | copy-start | bytes 24580
  6.5 6.7 %copy-start.2 = (s32[2048,1]{0,1:T(1,128)S(1)}, s32[2048,1]{0,1:T(1,128)}, u32[]{:S(2)}) copy-start(s32[2048,1]{0,1:T(1,128)} %param.19) | copy-start | bytes 24580
  6.5 6.7 %copy-start = (s32[2048]{0:T(1024)S(1)}, s32[2048]{0:T(1024)}, u32[]{:S(2)}) copy-start(s32[2048]{0:T(1024)} %param.20) | copy-start | bytes 24580
  6.5 158.3 %all-reduce.3.cloned.1.call-start = ((), (), s32[]{:S(2)}) async-start(), calls=%async_computation.2 | async-start | bytes 2097152
  9.3 4.0 %collective-permute-start = (bf16[16,4096]{1,0:T(8,128)(2,1)S(1)}, bf16[16,4096]{1,0:T(8,128)(2,1)S(1)}, u32[]{:S(2)}, u32[]{:S(2)}) collective-permute-start(bf16[16,4096]{1,0:T(8,128)(2,1)S(1)} %bitcast.66), channel_id=1, source_target_pairs={{0,1},{1,2},{2,3},{3,4},{4,5},{5,6},{6,7},{7,8},{8,9},{9,10},{10,1... | collective-permute-start | bytes 393224 | tf_op jit(solution)/shard_map/ppermute | solution.py:99
  11.2 5.3 %collective-permute-start.1 = (bf16[16,4096]{1,0:T(8,128)(2,1)S(1)}, bf16[16,4096]{1,0:T(8,128)(2,1)S(1)}, u32[]{:S(2)}, u32[]{:S(2)}) collective-permute-start(bf16[16,4096]{1,0:T(8,128)(2,1)S(1)} %bitcast.67), channel_id=1, source_target_pairs={{0,15},{1,0},{2,1},{3,2},{4,3},{5,4},{6,5},{7,6},{8,7},{9,8},{10,9... | collective-permute-start | bytes 393224 | tf_op jit(solution)/shard_map/ppermute | solution.py:104
  13.3 5.2 %collective-permute-start.2 = (bf16[16,4096]{1,0:T(8,128)(2,1)S(1)}, bf16[16,4096]{1,0:T(8,128)(2,1)S(1)}, u32[]{:S(2)}, u32[]{:S(2)}) collective-permute-start(bf16[16,4096]{1,0:T(8,128)(2,1)S(1)} %collective-permute-done), channel_id=1, source_target_pairs={{0,1},{1,2},{2,3},{3,4},{4,5},{5,6},{6,7},{7,8},{8,9},{9,10},{10,1... | collective-permute-start | bytes 393224 | tf_op jit(solution)/shard_map/ppermute | solution.py:99
  16.5 5.4 %collective-permute-start.3 = (bf16[16,4096]{1,0:T(8,128)(2,1)S(1)}, bf16[16,4096]{1,0:T(8,128)(2,1)S(1)}, u32[]{:S(2)}, u32[]{:S(2)}) collective-permute-start(bf16[16,4096]{1,0:T(8,128)(2,1)S(1)} %collective-permute-done.1), channel_id=1, source_target_pairs={{0,15},{1,0},{2,1},{3,2},{4,3},{5,4},{6,5},{7,6},{8,7},{9,8},{10,9... | collective-permute-start | bytes 393224 | tf_op jit(solution)/shard_map/ppermute | solution.py:104
  18.5 5.4 %collective-permute-start.4 = (bf16[16,4096]{1,0:T(8,128)(2,1)S(1)}, bf16[16,4096]{1,0:T(8,128)(2,1)S(1)}, u32[]{:S(2)}, u32[]{:S(2)}) collective-permute-start(bf16[16,4096]{1,0:T(8,128)(2,1)S(1)} %collective-permute-done.2), channel_id=1, source_target_pairs={{0,1},{1,2},{2,3},{3,4},{4,5},{5,6},{6,7},{7,8},{8,9},{9,10},{10,1... | collective-permute-start | bytes 393224 | tf_op jit(solution)/shard_map/ppermute | solution.py:99
  21.9 5.4 %collective-permute-start.5 = (bf16[16,4096]{1,0:T(8,128)(2,1)S(1)}, bf16[16,4096]{1,0:T(8,128)(2,1)S(1)}, u32[]{:S(2)}, u32[]{:S(2)}) collective-permute-start(bf16[16,4096]{1,0:T(8,128)(2,1)S(1)} %collective-permute-done.3), channel_id=1, source_target_pairs={{0,15},{1,0},{2,1},{3,2},{4,3},{5,4},{6,5},{7,6},{8,7},{9,8},{10,9... | collective-permute-start | bytes 393224 | tf_op jit(solution)/shard_map/ppermute | solution.py:104
  23.9 5.4 %collective-permute-start.6 = (bf16[16,4096]{1,0:T(8,128)(2,1)S(1)}, bf16[16,4096]{1,0:T(8,128)(2,1)S(1)}, u32[]{:S(2)}, u32[]{:S(2)}) collective-permute-start(bf16[16,4096]{1,0:T(8,128)(2,1)S(1)} %collective-permute-done.4), channel_id=1, source_target_pairs={{0,1},{1,2},{2,3},{3,4},{4,5},{5,6},{6,7},{7,8},{8,9},{9,10},{10,1... | collective-permute-start | bytes 393224 | tf_op jit(solution)/shard_map/ppermute | solution.py:99
  27.3 5.4 %collective-permute-start.7 = (bf16[16,4096]{1,0:T(8,128)(2,1)S(1)}, bf16[16,4096]{1,0:T(8,128)(2,1)S(1)}, u32[]{:S(2)}, u32[]{:S(2)}) collective-permute-start(bf16[16,4096]{1,0:T(8,128)(2,1)S(1)} %collective-permute-done.5), channel_id=1, source_target_pairs={{0,15},{1,0},{2,1},{3,2},{4,3},{5,4},{6,5},{7,6},{8,7},{9,8},{10,9... | collective-permute-start | bytes 393224 | tf_op jit(solution)/shard_map/ppermute | solution.py:104
  29.3 5.4 %collective-permute-start.8 = (bf16[16,4096]{1,0:T(8,128)(2,1)S(1)}, bf16[16,4096]{1,0:T(8,128)(2,1)S(1)}, u32[]{:S(2)}, u32[]{:S(2)}) collective-permute-start(bf16[16,4096]{1,0:T(8,128)(2,1)S(1)} %collective-permute-done.6), channel_id=1, source_target_pairs={{0,1},{1,2},{2,3},{3,4},{4,5},{5,6},{6,7},{7,8},{8,9},{9,10},{10,1... | collective-permute-start | bytes 393224 | tf_op jit(solution)/shard_map/ppermute | solution.py:99
  32.7 5.4 %collective-permute-start.9 = (bf16[16,4096]{1,0:T(8,128)(2,1)S(1)}, bf16[16,4096]{1,0:T(8,128)(2,1)S(1)}, u32[]{:S(2)}, u32[]{:S(2)}) collective-permute-start(bf16[16,4096]{1,0:T(8,128)(2,1)S(1)} %collective-permute-done.7), channel_id=1, source_target_pairs={{0,15},{1,0},{2,1},{3,2},{4,3},{5,4},{6,5},{7,6},{8,7},{9,8},{10,9... | collective-permute-start | bytes 393224 | tf_op jit(solution)/shard_map/ppermute | solution.py:104
  34.7 5.4 %collective-permute-start.10 = (bf16[16,4096]{1,0:T(8,128)(2,1)S(1)}, bf16[16,4096]{1,0:T(8,128)(2,1)S(1)}, u32[]{:S(2)}, u32[]{:S(2)}) collective-permute-start(bf16[16,4096]{1,0:T(8,128)(2,1)S(1)} %collective-permute-done.8), channel_id=1, source_target_pairs={{0,1},{1,2},{2,3},{3,4},{4,5},{5,6},{6,7},{7,8},{8,9},{9,10},{10,1... | collective-permute-start | bytes 393224 | tf_op jit(solution)/shard_map/ppermute | solution.py:99
  38.1 5.4 %collective-permute-start.11 = (bf16[16,4096]{1,0:T(8,128)(2,1)S(1)}, bf16[16,4096]{1,0:T(8,128)(2,1)S(1)}, u32[]{:S(2)}, u32[]{:S(2)}) collective-permute-start(bf16[16,4096]{1,0:T(8,128)(2,1)S(1)} %collective-permute-done.9), channel_id=1, source_target_pairs={{0,15},{1,0},{2,1},{3,2},{4,3},{5,4},{6,5},{7,6},{8,7},{9,8},{10,9... | collective-permute-start | bytes 393224 | tf_op jit(solution)/shard_map/ppermute | solution.py:104
  40.1 5.4 %collective-permute-start.12 = (bf16[16,4096]{1,0:T(8,128)(2,1)S(1)}, bf16[16,4096]{1,0:T(8,128)(2,1)S(1)}, u32[]{:S(2)}, u32[]{:S(2)}) collective-permute-start(bf16[16,4096]{1,0:T(8,128)(2,1)S(1)} %collective-permute-done.10), channel_id=1, source_target_pairs={{0,1},{1,2},{2,3},{3,4},{4,5},{5,6},{6,7},{7,8},{8,9},{9,10},{10,1... | collective-permute-start | bytes 393224 | tf_op jit(solution)/shard_map/ppermute | solution.py:99
  43.5 5.4 %collective-permute-start.13 = (bf16[16,4096]{1,0:T(8,128)(2,1)S(1)}, bf16[16,4096]{1,0:T(8,128)(2,1)S(1)}, u32[]{:S(2)}, u32[]{:S(2)}) collective-permute-start(bf16[16,4096]{1,0:T(8,128)(2,1)S(1)} %collective-permute-done.11), channel_id=1, source_target_pairs={{0,15},{1,0},{2,1},{3,2},{4,3},{5,4},{6,5},{7,6},{8,7},{9,8},{10,9... | collective-permute-start | bytes 393224 | tf_op jit(solution)/shard_map/ppermute | solution.py:104
  45.5 5.4 %collective-permute-start.14 = (bf16[16,4096]{1,0:T(8,128)(2,1)S(1)}, bf16[16,4096]{1,0:T(8,128)(2,1)S(1)}, u32[]{:S(2)}, u32[]{:S(2)}) collective-permute-start(bf16[16,4096]{1,0:T(8,128)(2,1)S(1)} %collective-permute-done.12), channel_id=1, source_target_pairs={{0,1},{1,2},{2,3},{3,4},{4,5},{5,6},{6,7},{7,8},{8,9},{9,10},{10,1... | collective-permute-start | bytes 393224 | tf_op jit(solution)/shard_map/ppermute | solution.py:99
  58.6 2.3 copy-start.4
  167.9 54.2 %all-to-all-start = ((bf16[16,16,4096]{2,1,0:T(8,128)(2,1)}), bf16[16,16,4096]{2,1,0:T(8,128)(2,1)S(1)}, u32[]{:S(2)}, u32[]{:S(2)}) async-start(bf16[16,16,4096]{2,1,0:T(8,128)(2,1)} %convolution_convert_fusion), calls=%async_computation | async-start | bytes 4194304 | tf_op jit(solution)/shard_map/all_to_all | solution.py:145
  235.1 97.4 %all-to-all-start.1 = ((f32[16,16,4096]{2,1,0:T(8,128)}), f32[16,16,4096]{2,1,0:T(8,128)}, u32[]{:S(2)}, u32[]{:S(2)}) async-start(f32[16,16,4096]{2,1,0:T(8,128)} %fusion.11), calls=%async_computation.1 | async-start | bytes 8388608 | tf_op jit(solution)/shard_map/all_to_all | solution.py:162
Sparse Core Ops, SparseCore 0:
  60.6 104.1 all-reduce.2
